TPU v7x, 256 devices: a whole 4x4x8 slice. The times are simulated.
256 devices in a mesh: seq: 64 (over z, x, core), tp: 4 (over y).
Axes of the slice: x: 4, y: 4, z: 8, core: 2. Of those that a mesh axis runs over, the one named last changes fastest.
Arguments:
- hidden: bfloat16 [32768, 4096], P(('seq', 'tp')), may hold values from -640 to 640
- norm_gain: float32 [4096], replicated, may hold values from 0.5 to 1.5
- w_query: bfloat16 [4096, 2048], P(None, 'tp'), may hold values from -0.078125 to 0.078125
- w_key: bfloat16 [4096, 1024], P(None, 'tp'), may hold values from -2.421875 to 2.421875
- w_value: bfloat16 [4096, 1024], P(None, 'tp'), may hold values from -0.09375 to 0.09375
- doc_start: int32 [32768], P('seq'), may hold values from 0 to 32767, as said below
- block_owner: int32 [1024], P('seq'), may hold values from 0 to 63, as said below
Outputs:
- context_rows: bfloat16 [32768, 2048], P(('seq', 'tp'))
- key_cache: bfloat16 [49152, 1024], P('seq', 'tp')
- value_cache: bfloat16 [49152, 1024], P('seq', 'tp')
Inputs may be any that keep to these rules, and one draw needn't show every extreme that they name: `doc_start`: rows with equal values form one document: consecutive rows beginning at the row whose number is that value. Every document has at most 256 rows and one has exactly 256; all but the last have at least 64. `block_owner`: owner numbers never fall along the blocks. Owner o holds the blocks from o * 16 + e(o) up to (o + 1) * 16 + e(o + 1) - 1, where -4 <= e <= 4 and e is 0 at both ends of the axis; so an owner holds between 8 and 24 blocks, and some owner holds exactly 24.
All inputs are finite; a program needn't handle non-finite values.
Results may differ from a plain program's by a relative error of at most 0.0078.
Values may be sent and summed in bfloat16 or wider, within the bound.
No kernel may reach another device: no remote copies, remote signals or barrier semaphores. Data moves between devices by JAX's collectives and lax.ppermute only.
A program may use at most 128 MiB of HBM per device.

v0:
```python
import jax
import jax.numpy as jnp
from jax import lax
from jax.sharding import PartitionSpec as P

HD = 128
DOC_MAX = 256
EPS = 1e-05
ROPE_BASE = 500000.0


def from_behind(array, axis, by):
    length = lax.axis_size(axis)
    pairs = [(i, i + by) for i in range(length) if 0 <= i + by < length]
    return lax.ppermute(array, axis, pairs)


def rotate(packed, positions, head_count):
    row_count = packed.shape[0]
    head_width = packed.shape[1] // head_count
    half_width = head_width // 2
    frequency = jnp.power(
        ROPE_BASE, -jnp.arange(half_width, dtype=jnp.float32) * (2.0 / head_width)
    )
    angles = positions.astype(jnp.float32)[:, None] * frequency[None, :]
    cosine = jnp.cos(angles)[:, None, :]
    sine_part = jnp.sin(angles)[:, None, :]
    reshaped = packed.reshape(row_count, head_count, head_width)
    first_half = reshaped[:, :, :half_width]
    second = reshaped[:, :, half_width:]
    rotated = jnp.concatenate(
        [first_half * cosine - second * sine_part, second * cosine + first_half * sine_part], axis=2
    )
    return rotated.reshape(row_count, head_count * head_width)


def project(rows_in, norm_gain, w_query, w_key, w_value, positions):
    widened = rows_in.astype(jnp.float32)
    inverse_rms = lax.rsqrt(jnp.mean(widened * widened, axis=1, keepdims=True) + EPS)
    normed = (widened * inverse_rms * norm_gain[None, :]).astype(jnp.bfloat16)
    queries = jnp.dot(normed, w_query, preferred_element_type=jnp.float32)
    keys_f = jnp.dot(normed, w_key, preferred_element_type=jnp.float32)
    values_f = jnp.dot(normed, w_value, preferred_element_type=jnp.float32)
    queries = rotate(queries, positions, queries.shape[1] // HD).astype(jnp.bfloat16)
    keys_f = rotate(keys_f, positions, keys_f.shape[1] // HD).astype(jnp.bfloat16)
    return (queries, keys_f, values_f.astype(jnp.bfloat16))


def attend(
    queries, keys_in, values_in, query_doc, query_row, key_doc, key_row, key_live, offset, reach
):
    row_count = queries.shape[0]
    groups = keys_in.shape[1] // HD
    per_group = queries.shape[1] // keys_in.shape[1]
    window = row_count + reach

    def one_tile(index):
        first = index * row_count
        key_first = first + offset - reach
        near_keys = lax.dynamic_slice_in_dim(keys_in, key_first, window, 0)
        near_values = lax.dynamic_slice_in_dim(values_in, key_first, window, 0)
        near_doc = lax.dynamic_slice_in_dim(key_doc, key_first, window, 0)
        near_row = lax.dynamic_slice_in_dim(key_row, key_first, window, 0)
        near_live = lax.dynamic_slice_in_dim(key_live, key_first, window, 0)
        query_four = queries.reshape(row_count, groups, per_group, HD)
        key_three = near_keys.reshape(window, groups, HD)
        value_three = near_values.reshape(window, groups, HD)
        scores = jnp.einsum(
            "rgjd,kgd->gjrk", query_four, key_three, preferred_element_type=jnp.float32
        ) * HD ** (-0.5)
        allowed = (
            (query_doc[:, None] == near_doc[None, :])
            & (near_row[None, :] <= query_row[:, None])
            & (near_live[None, :] > 0)
        )
        allowed = allowed | (jnp.arange(window)[None, :] == jnp.arange(row_count)[:, None] + reach)
        scores = jnp.where(allowed[None, None], scores, -jnp.inf)
        highest = jnp.max(scores, axis=3, keepdims=True)
        weights = jnp.exp(scores - highest)
        weights = (weights / jnp.sum(weights, axis=3, keepdims=True)).astype(jnp.bfloat16)
        blended = jnp.einsum(
            "gjrk,kgd->rgjd", weights, value_three, preferred_element_type=jnp.float32
        )
        return blended.astype(jnp.bfloat16).reshape(row_count, groups * per_group * HD)

    tiles = lax.map(one_tile, jnp.arange(row_count // row_count, dtype=jnp.int32))
    return tiles.reshape(row_count, queries.shape[1])


def shards(hidden, norm_gain, w_query, w_key, w_value, doc_start, block_owner):
    home_hidden = lax.all_gather(hidden, "tp", axis=0, tiled=True)
    my_index = lax.axis_index("seq")
    home_rows = home_hidden.shape[0]
    home_blocks = block_owner.shape[0]
    block_rows = home_rows // home_blocks
    spill_rows = home_blocks // 4 * block_rows
    frame_size = home_rows + 2 * spill_rows
    all_rows = lax.axis_size("seq") * home_rows
    row_number = my_index * home_rows + jnp.arange(home_rows, dtype=jnp.int32)
    row_owner = jnp.repeat(block_owner, block_rows)
    frame_number = my_index * home_rows - spill_rows + jnp.arange(frame_size, dtype=jnp.int32)
    queries, keys_own, values_own = project(
        home_hidden, norm_gain, w_query, w_key, w_value, row_number - doc_start
    )
    left = from_behind((keys_own, values_own, doc_start), "seq", 1)
    left_live = jnp.ones((home_rows,), jnp.int32) * (my_index > 0).astype(jnp.int32)
    home_context = attend(
        queries,
        jnp.concatenate([left[0], keys_own], axis=0),
        jnp.concatenate([left[1], values_own], axis=0),
        doc_start,
        row_number,
        jnp.concatenate([left[2], doc_start], axis=0),
        jnp.concatenate([row_number - home_rows, row_number], axis=0),
        jnp.concatenate([left_live, jnp.ones((home_rows,), jnp.int32)], axis=0),
        home_rows,
        DOC_MAX,
    )
    arrived = []
    for direction in (1, -1):
        low_row = home_rows - spill_rows if direction == 1 else 0
        payload = (
            keys_own[low_row : low_row + spill_rows],
            values_own[low_row : low_row + spill_rows],
            row_owner[low_row : low_row + spill_rows],
        )
        arrived.append(from_behind((payload[0], payload[1], payload[2]), "seq", direction))
    from_left, from_right = arrived
    frame_keys = jnp.concatenate([from_left[0], keys_own, from_right[0]], axis=0)
    frame_values = jnp.concatenate([from_left[1], values_own, from_right[1]], axis=0)
    frame_owner = jnp.concatenate([from_left[2], row_owner, from_right[2]], axis=0)
    frame_live = (
        (frame_owner == my_index) & (frame_number >= 0) & (frame_number < all_rows)
    ).astype(jnp.int32)
    live_column = frame_live[:, None] > 0
    key_cache = jnp.where(live_column, frame_keys, jnp.zeros((), jnp.bfloat16))
    value_cache = jnp.where(live_column, frame_values, jnp.zeros((), jnp.bfloat16))
    context_rows = lax.all_to_all(home_context, "tp", split_axis=0, concat_axis=1, tiled=True)
    return (context_rows, key_cache, value_cache)


def solution(mesh):
    return jax.shard_map(
        shards,
        mesh=mesh,
        in_specs=(
            P(("seq", "tp"), None),
            P(),
            P(None, "tp"),
            P(None, "tp"),
            P(None, "tp"),
            P("seq"),
            P("seq"),
        ),
        out_specs=(P(("seq", "tp"), None), P("seq", "tp"), P("seq", "tp")),
        check_vma=False,
    )
```

profile of v0, /device:TPU:128, one launch (start us, length us, event | category | flops | bytes accessed | tf_op | source)
XLA Modules:
  0.0 141.9 jit_solution(14735143676403520581)
XLA Ops:
  8.9 3.6 %collective-permute-start.4 = (s32[128]{0:T(128)S(1)}, s32[128]{0:T(128)S(1)}, u32[]{:S(2)}, u32[]{:S(2)}) collective-permute-start(s32[128]{0:T(128)S(1)} %slice.56), channel_id=1, source_target_pairs={{4,0},{8,4},{12,8},{16,12},{20,16},{24,20},{28,24},{32,28},{36,32}... | collective-permute-start | bytes 1544 | tf_op jit(solution)/shard_map/ppermute | solution.py:15
  12.7 1.9 %collective-permute-start.3 = (s32[128]{0:T(128)S(1)}, s32[128]{0:T(128)S(1)}, u32[]{:S(2)}, u32[]{:S(2)}) collective-permute-start(s32[128]{0:T(128)S(1)} %slice.54), channel_id=1, source_target_pairs={{0,4},{4,8},{8,12},{12,16},{16,20},{20,24},{24,28},{28,32},{32,36}... | collective-permute-start | bytes 1544 | tf_op jit(solution)/shard_map/ppermute | solution.py:15
  14.6 1.9 %collective-permute-start.1 = (s32[512]{0:T(512)}, s32[512]{0:T(512)S(1)}, u32[]{:S(2)}, u32[]{:S(2)}) collective-permute-start(s32[512]{0:T(512)} %param.12), channel_id=1, source_target_pairs={{0,4},{4,8},{8,12},{12,16},{16,20},{20,24},{24,28},{28,32},{32,36}... | collective-permute-start | bytes 6152 | tf_op jit(solution)/shard_map/ppermute | solution.py:15
  20.9 2.1 %collective-permute-done.1 = s32[512]{0:T(512)S(1)} collective-permute-done((s32[512]{0:T(512)}, s32[512]{0:T(512)S(1)}, u32[]{:S(2)}, u32[]{:S(2)}) %collective-permute-start.1) | collective-permute-done | bytes 2080 | tf_op jit(solution)/shard_map/ppermute | solution.py:15
  23.8 2.2 %fusion.9 = pred[512,768]{0,1:T(8,128)(4,1)} fusion(s32[512]{0:T(512)S(1)} %iota_add_fusion.1, s32[512]{0:T(512)S(1)} %get-tuple-element.62, s32[512]{0:T(512)} %param.12, s32[768]{0:T(1024)S(1)} %dynamic_slice.25, s32[768]{0:T(1024)S(1)} %dynamic_slice.24, pred[768]{0:T(1024)(128)(4,1)S(1)} %slice_compare_fusion), kind=kLoop, calls=%fused_computation.15 | loop fusion | flops 2359296 | bytes 406272 | tf_op jit(solution)/shard_map/while/body/eval_jaxpr/or | solution.py:76
  25.9 36.2 %all-gather.2.cloned.1.call-done = bf16[512,4096]{1,0:T(8,128)(2,1)} async-done(((bf16[128,4096]{1,0:T(8,128)(2,1)}), bf16[512,4096]{1,0:T(8,128)(2,1)}) %all-gather.2.cloned.1.call-update) | async-done | bytes 4194320 | tf_op jit(solution)/shard_map/all_gather | solution.py:91
  62.1 3.2 %fusion.1 = f32[512]{0:T(512)S(1)} fusion(bf16[512,4096]{1,0:T(8,128)(2,1)} %all-gather.2.cloned.1.call-done), kind=kLoop, calls=%fused_computation.3 | loop fusion | flops 6290944 | bytes 4196352 | tf_op jit(solution)/shard_map/reduce_sum | solution.py:39
  65.6 2.0 %convolution_convert_fusion = bf16[512,256]{1,0:T(8,128)(2,1)} fusion(bf16[4096,256]{1,0:T(8,128)(2,1)S(1)} %copy-done, bf16[512,4096]{1,0:T(8,128)(2,1)S(1)} %copy-done.1, f32[4096]{0:T(1024)S(1)} %copy-done.4, f32[512]{0:T(512)S(1)} %add_rsqrt_fusion), kind=kOutput, calls=%fused_computation.18 | convolution fusion | flops 1082261504 | bytes 6572032 | tf_op jit(solution)/shard_map/dot_general | solution.py:43
  68.5 1.9 %collective-permute-start = (bf16[512,256]{1,0:T(8,128)(2,1)}, bf16[512,256]{1,0:T(8,128)(2,1)}, u32[]{:S(2)}, u32[]{:S(2)}) collective-permute-start(bf16[512,256]{1,0:T(8,128)(2,1)} %convolution_convert_fusion), channel_id=1, source_target_pairs={{0,4},{4,8},{8,12},{12,16},{16,20},{20,24},{24,28},{28,32},{32,36}... | collective-permute-start | bytes 786440 | tf_op jit(solution)/shard_map/ppermute | solution.py:15
  70.5 3.5 %collective-permute-start.7 = (bf16[128,256]{1,0:T(8,128)(2,1)S(1)}, bf16[128,256]{1,0:T(8,128)(2,1)}, u32[]{:S(2)}, u32[]{:S(2)}) collective-permute-start(bf16[128,256]{1,0:T(8,128)(2,1)S(1)} %get-tuple-element.49), channel_id=1, source_target_pairs={{0,4},{4,8},{8,12},{12,16},{16,20},{20,24},{24,28},{28,32},{32,36}... | collective-permute-start | bytes 196616 | tf_op jit(solution)/shard_map/ppermute | solution.py:15
  73.9 5.4 %collective-permute-start.8 = (bf16[128,256]{1,0:T(8,128)(2,1)S(1)}, bf16[128,256]{1,0:T(8,128)(2,1)}, u32[]{:S(2)}, u32[]{:S(2)}) collective-permute-start(bf16[128,256]{1,0:T(8,128)(2,1)S(1)} %get-tuple-element.50), channel_id=1, source_target_pairs={{4,0},{8,4},{12,8},{16,12},{20,16},{24,20},{28,24},{32,28},{36,32}... | collective-permute-start | bytes 196616 | tf_op jit(solution)/shard_map/ppermute | solution.py:15
  79.4 1.6 %fusion.30 = f32[512,256]{0,1:T(8,128)S(1)} fusion(bf16[4096,256]{1,0:T(8,128)(2,1)S(1)} %copy-done.3, bf16[512,4096]{1,0:T(8,128)(2,1)S(1)} %copy-done.1, f32[4096]{0:T(1024)S(1)} %copy-done.4, f32[512]{0:T(512)S(1)} %add_rsqrt_fusion), kind=kOutput, calls=%fused_computation.59 | convolution fusion | flops 1082130432 | bytes 6834176 | tf_op jit(solution)/shard_map/dot_general | solution.py:42
  82.0 1.2 copy.45
  83.2 1.6 %subtract_convert_fusion.1 = (bf16[512,2,64]{2,1,0:T(2,128)(2,1)S(1)}, bf16[512,2,64]{2,1,0:T(2,128)(2,1)S(1)}) fusion(f32[512,2,64]{2,1,0:T(2,128)S(1)} %copy.46, f32[512,2,64]{2,1,0:T(2,128)S(1)} %copy.45, f32[512,64]{1,0:T(8,128)} %copy.32, f32[512,64]{1,0:T(8,128)} %copy.30), kind=kLoop, calls=%fused_computation.24 | loop fusion | flops 524288 | bytes 1048576 | tf_op jit(solution)/shard_map/convert.2
  85.5 1.9 %collective-permute-start.2 = (bf16[512,256]{1,0:T(8,128)(2,1)S(1)}, bf16[512,256]{1,0:T(8,128)(2,1)S(1)}, u32[]{:S(2)}, u32[]{:S(2)}) collective-permute-start(bf16[512,256]{1,0:T(8,128)(2,1)S(1)} %bitcast.51), channel_id=1, source_target_pairs={{0,4},{4,8},{8,12},{12,16},{16,20},{20,24},{24,28},{28,32},{32,36}... | collective-permute-start | bytes 786440 | tf_op jit(solution)/shard_map/ppermute | solution.py:15
  87.4 5.9 %fusion.28 = f32[512,512]{0,1:T(8,128)S(1)} fusion(bf16[4096,512]{1,0:T(8,128)(2,1)} %param.9, bf16[512,4096]{1,0:T(8,128)(2,1)} %all-gather.2.cloned.1.call-done, f32[4096]{0:T(1024)} %param.8, f32[512]{0:T(512)S(1)} %add_rsqrt_fusion), kind=kOutput, calls=%fused_computation.58 | convolution fusion | flops 2155872256 | bytes 9455616 | tf_op jit(solution)/shard_map/dot_general | solution.py:41
  94.0 7.0 %collective-permute-start.6 = (bf16[128,256]{1,0:T(8,128)(2,1)S(1)}, bf16[128,256]{1,0:T(8,128)(2,1)S(1)}, u32[]{:S(2)}, u32[]{:S(2)}) collective-permute-start(bf16[128,256]{1,0:T(8,128)(2,1)S(1)} %bitcast.60), channel_id=1, source_target_pairs={{4,0},{8,4},{12,8},{16,12},{20,16},{24,20},{28,24},{32,28},{36,32}... | collective-permute-start | bytes 196616 | tf_op jit(solution)/shard_map/ppermute | solution.py:15
  100.9 2.1 %collective-permute-start.5 = (bf16[128,256]{1,0:T(8,128)(2,1)S(1)}, bf16[128,256]{1,0:T(8,128)(2,1)S(1)}, u32[]{:S(2)}, u32[]{:S(2)}) collective-permute-start(bf16[128,256]{1,0:T(8,128)(2,1)S(1)} %bitcast.59), channel_id=1, source_target_pairs={{0,4},{4,8},{8,12},{12,16},{16,20},{20,24},{24,28},{28,32},{32,36}... | collective-permute-start | bytes 196616 | tf_op jit(solution)/shard_map/ppermute | solution.py:15
  103.1 6.7 %collective-permute-done.5 = bf16[128,256]{1,0:T(8,128)(2,1)S(1)} collective-permute-done((bf16[128,256]{1,0:T(8,128)(2,1)S(1)}, bf16[128,256]{1,0:T(8,128)(2,1)S(1)}, u32[]{:S(2)}, u32[]{:S(2)}) %collective-permute-start.5) | collective-permute-done | bytes 65568 | tf_op jit(solution)/shard_map/ppermute | solution.py:15
  109.9 2.3 %maximum_select_fusion.1 = (bf16[768,256]{1,0:T(8,128)(2,1)}, bf16[768,256]{1,0:T(8,128)(2,1)S(1)}, bf16[768,256]{1,0:T(8,128)(2,1)S(1)}, bf16[768,256]{1,0:T(8,128)(2,1)}) fusion(bf16[128,256]{1,0:T(8,128)(2,1)} %collective-permute-done.8, bf16[512,256]{1,0:T(8,128)(2,1)} %convolution_convert_fusion, bf16[128,256]{1,0:T(8,128)(2,1)} %collective-permute-done.7, ...), kind=kLoop, calls=%fused_computation.28 | loop fusion | flops 4325376 | bytes 2884352 | tf_op jit(solution)/shard_map/jit(_where)/select_n | solution.py:137
  113.2 6.1 %fusion.36 = (f32[2,2,512]{2,1,0:T(2,128)S(1)}, f32[2,2,512,768]{2,3,1,0:T(8,128)}) fusion(pred[512,768]{0,1:T(8,128)(4,1)} %fusion.9, bf16[512,2,2,128]{0,3,2,1:T(8,128)(2,1)S(1)} %bitcast.53, bf16[768,2,128,1]{2,1,0,3:T(2,128)(2,1)S(1)} %bitcast.56), kind=kOutput, calls=%fused_computation.63 | convolution fusion | flops 408945408 | bytes 7610368 | tf_op jit(solution)/shard_map/while/body/eval_jaxpr/sub | solution.py:79
  119.3 3.4 %fusion.11 = bf16[512,2,2,128]{0,3,2,1:T(8,128)(2,1)S(1)} fusion(bf16[768,2,128,1]{0,2,3,1:T(8,128)(2,1)S(1)} %bitcast.55, f32[2,2,512,768]{2,3,1,0:T(8,128)} %get-tuple-element.60, f32[2,2,512]{2,1,0:T(2,128)S(1)} %get-tuple-element.59), kind=kOutput, calls=%fused_computation.17 | convolution fusion | flops 406061056 | bytes 7217152 | tf_op jit(solution)/shard_map/while/body/eval_jaxpr/gjrk,kgd->rgjd/dot_general | solution.py:81
  122.9 11.2 %all_to_all.19 = bf16[4,128,512]{1,2,0:T(8,128)(2,1)S(1)} all-to-all(bf16[4,128,512]{1,2,0:T(8,128)(2,1)S(1)} %copy.37), channel_id=1, replica_groups=mesh['seq'=64,'tp'=4] {'tp'}, dimensions={0} | all-to-all | bytes 1048576 | tf_op jit(solution)/shard_map/all_to_all | solution.py:138
  134.1 1.0 copy.38
  (55 shorter events, 11.5 us)
Async XLA Ops:
  7.2 58.2 %copy-start = (bf16[4096,256]{1,0:T(8,128)(2,1)S(1)}, bf16[4096,256]{1,0:T(8,128)(2,1)}, u32[]{:S(2)}) copy-start(bf16[4096,256]{1,0:T(8,128)(2,1)} %param.11) | copy-start | bytes 6291460
  7.2 58.2 %copy-start.4 = (f32[4096]{0:T(1024)S(1)}, f32[4096]{0:T(1024)}, u32[]{:S(2)}) copy-start(f32[4096]{0:T(1024)} %param.8) | copy-start | bytes 49156
  7.2 54.9 %all-gather.2.cloned.1.call-start = ((), (), s32[]{:S(2)}) async-start(), calls=%async_computation.1 | async-start | bytes 5242880 | tf_op jit(solution)/shard_map/all_gather | solution.py:91
  8.9 11.4 %collective-permute-start.4 = (s32[128]{0:T(128)S(1)}, s32[128]{0:T(128)S(1)}, u32[]{:S(2)}, u32[]{:S(2)}) collective-permute-start(s32[128]{0:T(128)S(1)} %slice.56), channel_id=1, source_target_pairs={{4,0},{8,4},{12,8},{16,12},{20,16},{24,20},{28,24},{32,28},{36,32}... | collective-permute-start | bytes 1544 | tf_op jit(solution)/shard_map/ppermute | solution.py:15
  12.7 8.2 %collective-permute-start.3 = (s32[128]{0:T(128)S(1)}, s32[128]{0:T(128)S(1)}, u32[]{:S(2)}, u32[]{:S(2)}) collective-permute-start(s32[128]{0:T(128)S(1)} %slice.54), channel_id=1, source_target_pairs={{0,4},{4,8},{8,12},{12,16},{16,20},{20,24},{24,28},{28,32},{32,36}... | collective-permute-start | bytes 1544 | tf_op jit(solution)/shard_map/ppermute | solution.py:15
  14.6 8.4 %collective-permute-start.1 = (s32[512]{0:T(512)}, s32[512]{0:T(512)S(1)}, u32[]{:S(2)}, u32[]{:S(2)}) collective-permute-start(s32[512]{0:T(512)} %param.12), channel_id=1, source_target_pairs={{0,4},{4,8},{8,12},{12,16},{16,20},{20,24},{24,28},{28,32},{32,36}... | collective-permute-start | bytes 6152 | tf_op jit(solution)/shard_map/ppermute | solution.py:15
  62.1 3.4 %copy-start.1 = (bf16[512,4096]{1,0:T(8,128)(2,1)S(1)}, bf16[512,4096]{1,0:T(8,128)(2,1)}, u32[]{:S(2)}) copy-start(bf16[512,4096]{1,0:T(8,128)(2,1)} %all-gather.2.cloned.1.call-done) | copy-start | bytes 12582916
  65.6 13.8 %copy-start.3 = (bf16[4096,256]{1,0:T(8,128)(2,1)S(1)}, bf16[4096,256]{1,0:T(8,128)(2,1)}, u32[]{:S(2)}) copy-start(bf16[4096,256]{1,0:T(8,128)(2,1)} %param.10) | copy-start | bytes 6291460
  68.5 41.3 %collective-permute-start = (bf16[512,256]{1,0:T(8,128)(2,1)}, bf16[512,256]{1,0:T(8,128)(2,1)}, u32[]{:S(2)}, u32[]{:S(2)}) collective-permute-start(bf16[512,256]{1,0:T(8,128)(2,1)} %convolution_convert_fusion), channel_id=1, source_target_pairs={{0,4},{4,8},{8,12},{12,16},{16,20},{20,24},{24,28},{28,32},{32,36}... | collective-permute-start | bytes 786440 | tf_op jit(solution)/shard_map/ppermute | solution.py:15
  70.5 30.5 %collective-permute-start.7 = (bf16[128,256]{1,0:T(8,128)(2,1)S(1)}, bf16[128,256]{1,0:T(8,128)(2,1)}, u32[]{:S(2)}, u32[]{:S(2)}) collective-permute-start(bf16[128,256]{1,0:T(8,128)(2,1)S(1)} %get-tuple-element.49), channel_id=1, source_target_pairs={{0,4},{4,8},{8,12},{12,16},{16,20},{20,24},{24,28},{28,32},{32,36}... | collective-permute-start | bytes 196616 | tf_op jit(solution)/shard_map/ppermute | solution.py:15
  73.9 29.2 %collective-permute-start.8 = (bf16[128,256]{1,0:T(8,128)(2,1)S(1)}, bf16[128,256]{1,0:T(8,128)(2,1)}, u32[]{:S(2)}, u32[]{:S(2)}) collective-permute-start(bf16[128,256]{1,0:T(8,128)(2,1)S(1)} %get-tuple-element.50), channel_id=1, source_target_pairs={{4,0},{8,4},{12,8},{16,12},{20,16},{24,20},{28,24},{32,28},{36,32}... | collective-permute-start | bytes 196616 | tf_op jit(solution)/shard_map/ppermute | solution.py:15
  85.5 24.4 %collective-permute-start.2 = (bf16[512,256]{1,0:T(8,128)(2,1)S(1)}, bf16[512,256]{1,0:T(8,128)(2,1)S(1)}, u32[]{:S(2)}, u32[]{:S(2)}) collective-permute-start(bf16[512,256]{1,0:T(8,128)(2,1)S(1)} %bitcast.51), channel_id=1, source_target_pairs={{0,4},{4,8},{8,12},{12,16},{16,20},{20,24},{24,28},{28,32},{32,36}... | collective-permute-start | bytes 786440 | tf_op jit(solution)/shard_map/ppermute | solution.py:15
  94.0 9.1 %collective-permute-start.6 = (bf16[128,256]{1,0:T(8,128)(2,1)S(1)}, bf16[128,256]{1,0:T(8,128)(2,1)S(1)}, u32[]{:S(2)}, u32[]{:S(2)}) collective-permute-start(bf16[128,256]{1,0:T(8,128)(2,1)S(1)} %bitcast.60), channel_id=1, source_target_pairs={{4,0},{8,4},{12,8},{16,12},{20,16},{24,20},{28,24},{32,28},{36,32}... | collective-permute-start | bytes 196616 | tf_op jit(solution)/shard_map/ppermute | solution.py:15
  100.9 8.9 %collective-permute-start.5 = (bf16[128,256]{1,0:T(8,128)(2,1)S(1)}, bf16[128,256]{1,0:T(8,128)(2,1)S(1)}, u32[]{:S(2)}, u32[]{:S(2)}) collective-permute-start(bf16[128,256]{1,0:T(8,128)(2,1)S(1)} %bitcast.59), channel_id=1, source_target_pairs={{0,4},{4,8},{8,12},{12,16},{16,20},{20,24},{24,28},{28,32},{32,36}... | collective-permute-start | bytes 196616 | tf_op jit(solution)/shard_map/ppermute | solution.py:15
  113.2 6.1 %copy-start.2 = (bf16[768,256]{0,1:T(8,128)(2,1)S(1)}, bf16[768,256]{0,1:T(8,128)(2,1)}, u32[]{:S(2)}) copy-start(bf16[768,256]{0,1:T(8,128)(2,1)} %copy.42) | copy-start | bytes 1179652
Sparse Core Ops, SparseCore 0:
  9.8 52.2 all-gather.1
where the time goes:
time: 143 us; the launch traced here: 142 us
  waiting for transfers between devices  46.3 us (32%)
  starting transfers between devices  29.3 us (20%)
  matrix products  19.1 us (13%)
  between operations  14.4 us (10%)
  other arithmetic  12.5 us (9%)
  blocking collectives  11.2 us (8%)
  local copies, waits for them, and re-layouts  9.14 us (6%)
    all_gather x1, waiting for transfers between devices, shards(): home_hidden = lax.all_gather(hidden, 'tp', axis=0, tiled=True)  36.2 us
    ppermute x9, starting transfers between devices, from_behind(): return lax.ppermute(array, axis, pairs)  29.3 us
    all_to_all x1, blocking collectives, shards(): lax.all_to_all(home_context, 'tp', split_axis=0, concat_axis=1, tiled=True)  11.2 us
    ppermute x9, waiting for transfers between devices, from_behind(): return lax.ppermute(array, axis, pairs)  9.44 us
    sub x1, matrix products, one_tile(): weights = jnp.exp(scores - highest)  6.09 us
    dot_general x1, matrix products, project(): queries = jnp.dot(normed, w_query, preferred_element_type=jnp.float32)  5.94 us
    dot_general x1, matrix products, one_tile(): jnp.einsum('gjrk,kgd->rgjd', weights, value_three, preferred_element_type...  3.37 us
    reduce_sum x1, other arithmetic, project(): jnp.mean(widened * widened, axis=1, keepdims=True) + EPS  3.23 us
  transfers between devices with their start and end apart: 10, of which 4 were waited for; matrix products, arithmetic and copies ran while one was open for 14% of the time, Pallas kernels for 0%

commit v1 on v0

--- a/solution.py
+++ b/solution.py
@@ -2,6 +2,7 @@
 import jax.numpy as jnp
 from jax import lax
 from jax.sharding import PartitionSpec as P
+from jax.lax import all_to_all, axis_size
 
 HD = 128
 DOC_MAX = 256
@@ -88,7 +89,12 @@
 
 
 def shards(hidden, norm_gain, w_query, w_key, w_value, doc_start, block_owner):
-    home_hidden = lax.all_gather(hidden, "tp", axis=0, tiled=True)
+
+    def arrange_series_all(w_in):
+        m_next = jnp.stack([w_in for _ in range(axis_size("tp"))])
+        return jnp.concatenate(all_to_all(m_next, "tp", 0, 0), 0)
+
+    home_hidden = arrange_series_all(hidden)
     my_index = lax.axis_index("seq")
     home_rows = home_hidden.shape[0]
     home_blocks = block_owner.shape[0]

time: 143 us -> 133 us (0.930)
  between operations: 14.4 us -> 1 us
  waiting for transfers between devices: 46.3 us -> 34.4 us
  local copies, waits for them, and re-layouts: 9.14 us -> 18 us
  starting transfers between devices: 29.3 us -> 34.2 us
  other arithmetic: 12.5 us -> 16.2 us
    all_gather x1 -> x0, waiting for transfers between devices: 36.2 us -> none  [shards(): home_hidden = lax.all_gather(hidden, 'tp', axis=0, tiled=True)]
    all_to_all x0 -> x1, waiting for transfers between devices: none -> 28.4 us  [arrange_series_all(): return jnp.concatenate(all_to_all(m_next, 'tp', 0, 0), 0)]
    dot_general x0 -> x2, local copies, waits for them, and re-layouts: none -> 10.5 us  [the longest x1 6.39 us: project(): queries = jnp.dot(normed, w_query, preferred_element_type=jnp.float32)]
    convert_element_type x0 -> x2, other arithmetic: none -> 7.79 us  [project(): normed = (widened * inverse_rms * norm_gain[None, :]).astype(jnp.bfloat16)]
    all_to_all x0 -> x1, starting transfers between devices: none -> 4.97 us  [arrange_series_all(): return jnp.concatenate(all_to_all(m_next, 'tp', 0, 0), 0)]
    another operation x0 -> x1, local copies, waits for them, and re-layouts: none -> 3.85 us  [arrange_series_all(): m_next = jnp.stack([w_in for _ in range(axis_size('tp'))])]
    ppermute x9, waiting for transfers between devices: 9.44 us -> 5.98 us  [from_behind(): return lax.ppermute(array, axis, pairs)]
    another operation x2, other arithmetic: 1.76 us -> 0.27 us
  transfers between devices with their start and end apart: 10 -> 10, of which waited for: 4 -> 2; matrix products, arithmetic and copies ran while one was open for 14% -> 19% of each run, Pallas kernels for 0% -> 0%
where the time goes in v1:
time: 133 us; the launch traced here: 132 us
  waiting for transfers between devices  34.4 us (26%)
  starting transfers between devices  34.2 us (26%)
  local copies, waits for them, and re-layouts  18 us (14%)
  matrix products  17.9 us (13%)
  other arithmetic  16.2 us (12%)
  blocking collectives  10.5 us (8%)
    ppermute x9, starting transfers between devices, from_behind(): return lax.ppermute(array, axis, pairs)  29.3 us
    all_to_all x1, waiting for transfers between devices, arrange_series_all(): return jnp.concatenate(all_to_all(m_next, 'tp', 0, 0), 0)  28.4 us
    all_to_all x1, blocking collectives, shards(): lax.all_to_all(home_context, 'tp', split_axis=0, concat_axis=1, tiled=True)  10.5 us
    convert_element_type x2, other arithmetic, project(): normed = (widened * inverse_rms * norm_gain[None, :]).astype(jnp.bfloat16)  7.79 us
    dot_general x1, local copies, waits for them, and re-layouts, project(): queries = jnp.dot(normed, w_query, preferred_element_type=jnp.float32)  6.39 us
    sub x1, matrix products, one_tile(): weights = jnp.exp(scores - highest)  6.17 us
    ppermute x9, waiting for transfers between devices, from_behind(): return lax.ppermute(array, axis, pairs)  5.98 us
    dot_general x1, matrix products, project(): queries = jnp.dot(normed, w_query, preferred_element_type=jnp.float32)  5.83 us
  transfers between devices with their start and end apart: 10, of which 2 were waited for; matrix products, arithmetic and copies ran while one was open for 19% of the time, Pallas kernels for 0%

profile of v1, /device:TPU:128, one launch (start us, length us, event | category | flops | bytes accessed | tf_op | source)
XLA Modules:
  0.0 132.2 jit_solution(12077392854586512323)
XLA Ops:
  0.6 3.8 %stack.2 = bf16[4,128,4096]{2,1,0:T(8,128)(2,1)} broadcast(bf16[128,4096]{1,0:T(8,128)(2,1)} %param.7), dimensions={1,2} | broadcast | bytes 5242880 | tf_op jit(solution)/shard_map/stack | solution.py:94
  4.5 5.0 %all-to-all-start = ((bf16[4,128,4096]{2,1,0:T(8,128)(2,1)}), bf16[4,128,4096]{2,1,0:T(8,128)(2,1)}, u32[]{:S(2)}, u32[]{:S(2)}) async-start(bf16[4,128,4096]{2,1,0:T(8,128)(2,1)} %stack.2), calls=%async_computation | async-start | bytes 8388608 | tf_op jit(solution)/shard_map/all_to_all | solution.py:95
  9.7 3.6 %collective-permute-start.4 = (s32[128]{0:T(128)S(1)}, s32[128]{0:T(128)S(1)}, u32[]{:S(2)}, u32[]{:S(2)}) collective-permute-start(s32[128]{0:T(128)S(1)} %slice.56), channel_id=1, source_target_pairs={{4,0},{8,4},{12,8},{16,12},{20,16},{24,20},{28,24},{32,28},{36,32}... | collective-permute-start | bytes 1544 | tf_op jit(solution)/shard_map/ppermute | solution.py:16
  13.5 1.9 %collective-permute-start.3 = (s32[128]{0:T(128)S(1)}, s32[128]{0:T(128)S(1)}, u32[]{:S(2)}, u32[]{:S(2)}) collective-permute-start(s32[128]{0:T(128)S(1)} %slice.54), channel_id=1, source_target_pairs={{0,4},{4,8},{8,12},{12,16},{16,20},{20,24},{24,28},{28,32},{32,36}... | collective-permute-start | bytes 1544 | tf_op jit(solution)/shard_map/ppermute | solution.py:16
  15.5 1.9 %collective-permute-start.1 = (s32[512]{0:T(512)S(1)}, s32[512]{0:T(512)S(1)}, u32[]{:S(2)}, u32[]{:S(2)}) collective-permute-start(s32[512]{0:T(512)S(1)} %copy-done.4), channel_id=1, source_target_pairs={{0,4},{4,8},{8,12},{12,16},{16,20},{20,24},{24,28},{28,32},{32,36}... | collective-permute-start | bytes 6152 | tf_op jit(solution)/shard_map/ppermute | solution.py:16
  18.2 4.1 %copy.36 = bf16[256,4096]{1,0:T(8,128)(2,1)} copy(bf16[256,4096]{0,1:T(8,128)(2,1)} %bitcast.58) | data formatting | bytes 4194304 | tf_op jit(solution)/shard_map/dot_general | solution.py:43
  22.3 6.4 %copy.40 = bf16[512,4096]{1,0:T(8,128)(2,1)} copy(bf16[512,4096]{0,1:T(8,128)(2,1)} %bitcast.56) | data formatting | bytes 8388608 | tf_op jit(solution)/shard_map/dot_general | solution.py:42
  28.7 1.5 %fusion.8 = pred[512,768]{0,1:T(8,128)(4,1)} fusion(s32[512]{0:T(512)S(1)} %iota_add_fusion.1, s32[512]{0:T(512)S(1)} %get-tuple-element.59, s32[512]{0:T(512)S(1)} %copy-done.4, s32[768]{0:T(1024)S(1)} %dynamic_slice.25, s32[768]{0:T(1024)S(1)} %dynamic_slice.24, pred[768]{0:T(1024)(128)(4,1)S(1)} %slice_compare_fusion), kind=kLoop, calls=%fused_computation.15 | loop fusion | flops 2359296 | bytes 406272 | tf_op jit(solution)/shard_map/while/body/eval_jaxpr/or | solution.py:77
  30.2 28.4 %all-to-all-done = bf16[4,128,4096]{2,1,0:T(8,128)(2,1)} async-done(((bf16[4,128,4096]{2,1,0:T(8,128)(2,1)}), bf16[4,128,4096]{2,1,0:T(8,128)(2,1)}, u32[]{:S(2)}, u32[]{:S(2)}) %all-to-all-start) | async-done | bytes 4194336 | tf_op jit(solution)/shard_map/all_to_all | solution.py:95
  58.6 3.1 %multiply_reduce_fusion = f32[4,128]{1,0:T(4,128)S(1)} fusion(bf16[4,128,4096]{2,1,0:T(8,128)(2,1)} %all-to-all-done), kind=kLoop, calls=%fused_computation.5 | loop fusion | flops 6290944 | bytes 4196352 | tf_op jit(solution)/shard_map/reduce_sum | solution.py:40
  61.7 3.8 %fusion.2 = bf16[512,4096]{1,0:T(8,128)(2,1)S(1)} fusion(bf16[4,128,4096]{2,1,0:T(8,128)(2,1)} %all-to-all-done, f32[4096]{0:T(1024)S(1)} %copy-done.3, f32[512]{0:T(512)S(1)} %get-tuple-element.51), kind=kLoop, calls=%fused_computation.3 | loop fusion | flops 8388608 | bytes 8407040 | tf_op jit(solution)/shard_map/convert_element_type | solution.py:41
  67.5 1.9 %collective-permute-start = (bf16[512,256]{1,0:T(8,128)(2,1)S(1)}, bf16[512,256]{1,0:T(8,128)(2,1)}, u32[]{:S(2)}, u32[]{:S(2)}) collective-permute-start(bf16[512,256]{1,0:T(8,128)(2,1)S(1)} %convolution_convert_fusion), channel_id=1, source_target_pairs={{0,4},{4,8},{8,12},{12,16},{16,20},{20,24},{24,28},{28,32},{32,36}... | collective-permute-start | bytes 786440 | tf_op jit(solution)/shard_map/ppermute | solution.py:16
  69.4 4.0 %multiply_convert_fusion = bf16[4,128,4096]{2,1,0:T(8,128)(2,1)S(1)} fusion(bf16[4,128,4096]{2,1,0:T(8,128)(2,1)} %all-to-all-done, f32[4096]{0:T(1024)S(1)} %copy-done.3, f32[4,128]{1,0:T(4,128)S(1)} %get-tuple-element.50), kind=kLoop, calls=%fused_computation.4 | loop fusion | flops 8388608 | bytes 8407040 | tf_op jit(solution)/shard_map/convert_element_type | solution.py:41
  75.4 7.0 %collective-permute-start.8 = (bf16[128,256]{1,0:T(8,128)(2,1)}, bf16[128,256]{1,0:T(8,128)(2,1)}, u32[]{:S(2)}, u32[]{:S(2)}) collective-permute-start(bf16[128,256]{1,0:T(8,128)(2,1)} %get-tuple-element.43), channel_id=1, source_target_pairs={{4,0},{8,4},{12,8},{16,12},{20,16},{24,20},{28,24},{32,28},{36,32}... | collective-permute-start | bytes 196616 | tf_op jit(solution)/shard_map/ppermute | solution.py:16
  82.4 1.9 %collective-permute-start.7 = (bf16[128,256]{1,0:T(8,128)(2,1)}, bf16[128,256]{1,0:T(8,128)(2,1)}, u32[]{:S(2)}, u32[]{:S(2)}) collective-permute-start(bf16[128,256]{1,0:T(8,128)(2,1)} %get-tuple-element.42), channel_id=1, source_target_pairs={{0,4},{4,8},{8,12},{12,16},{16,20},{20,24},{24,28},{28,32},{32,36}... | collective-permute-start | bytes 196616 | tf_op jit(solution)/shard_map/ppermute | solution.py:16
  84.5 1.9 %collective-permute-start.2 = (bf16[512,256]{1,0:T(8,128)(2,1)S(1)}, bf16[512,256]{1,0:T(8,128)(2,1)}, u32[]{:S(2)}, u32[]{:S(2)}) collective-permute-start(bf16[512,256]{1,0:T(8,128)(2,1)S(1)} %copy.37), channel_id=1, source_target_pairs={{0,4},{4,8},{8,12},{12,16},{16,20},{20,24},{24,28},{28,32},{32,36}... | collective-permute-start | bytes 786440 | tf_op jit(solution)/shard_map/ppermute | solution.py:16
  86.5 7.0 %collective-permute-start.6 = (bf16[128,256]{1,0:T(8,128)(2,1)S(1)}, bf16[128,256]{1,0:T(8,128)(2,1)}, u32[]{:S(2)}, u32[]{:S(2)}) collective-permute-start(bf16[128,256]{1,0:T(8,128)(2,1)S(1)} %copy.42), channel_id=1, source_target_pairs={{4,0},{8,4},{12,8},{16,12},{20,16},{24,20},{28,24},{32,28},{36,32}... | collective-permute-start | bytes 196616 | tf_op jit(solution)/shard_map/ppermute | solution.py:16
  93.5 5.8 %fusion.38 = f32[512,4,128]{0,2,1:T(8,128)S(1)} fusion(bf16[512,4096,1]{1,0,2:T(8,128)(2,1)} %bitcast.55, bf16[4,128,4096]{2,1,0:T(8,128)(2,1)} %bitcast.57), kind=kOutput, calls=%fused_computation.64 | convolution fusion | flops 2147483648 | bytes 9437184 | tf_op jit(solution)/shard_map/dot_general | solution.py:42
  99.6 2.1 %collective-permute-start.5 = (bf16[128,256]{1,0:T(8,128)(2,1)S(1)}, bf16[128,256]{1,0:T(8,128)(2,1)S(1)}, u32[]{:S(2)}, u32[]{:S(2)}) collective-permute-start(bf16[128,256]{1,0:T(8,128)(2,1)S(1)} %copy.41), channel_id=1, source_target_pairs={{0,4},{4,8},{8,12},{12,16},{16,20},{20,24},{24,28},{28,32},{32,36}... | collective-permute-start | bytes 196616 | tf_op jit(solution)/shard_map/ppermute | solution.py:16
  102.6 6.0 %collective-permute-done.5 = bf16[128,256]{1,0:T(8,128)(2,1)S(1)} collective-permute-done((bf16[128,256]{1,0:T(8,128)(2,1)S(1)}, bf16[128,256]{1,0:T(8,128)(2,1)S(1)}, u32[]{:S(2)}, u32[]{:S(2)}) %collective-permute-start.5) | collective-permute-done | bytes 65568 | tf_op jit(solution)/shard_map/ppermute | solution.py:16
  108.5 2.2 %maximum_select_fusion.1 = (bf16[768,256]{1,0:T(8,128)(2,1)}, bf16[768,256]{1,0:T(8,128)(2,1)S(1)}, bf16[768,256]{1,0:T(8,128)(2,1)S(1)}, bf16[768,256]{1,0:T(8,128)(2,1)}) fusion(bf16[128,256]{1,0:T(8,128)(2,1)} %collective-permute-done.8, bf16[512,256]{1,0:T(8,128)(2,1)S(1)} %convolution_convert_fusion, bf16[128,256]{1,0:T(8,128)(2,1)} %collective-permute-done.7, ...), kind=kLoop, calls=%fused_computation.26 | loop fusion | flops 4325376 | bytes 2884352 | tf_op jit(solution)/shard_map/jit(_where)/select_n | solution.py:143
  111.0 6.2 %fusion.32 = (f32[2,2,512]{2,1,0:T(2,128)S(1)}, f32[2,2,512,768]{2,3,1,0:T(8,128)}) fusion(pred[512,768]{0,1:T(8,128)(4,1)} %fusion.8, bf16[512,2,2,128]{0,3,2,1:T(8,128)(2,1)} %bitcast.62, bf16[768,2,128,1]{2,1,0,3:T(2,128)(2,1)S(1)} %bitcast.64), kind=kOutput, calls=%fused_computation.62 | convolution fusion | flops 408945408 | bytes 7610368 | tf_op jit(solution)/shard_map/while/body/eval_jaxpr/sub | solution.py:80
  117.1 3.4 %fusion.10 = bf16[512,2,2,128]{0,3,2,1:T(8,128)(2,1)S(1)} fusion(bf16[768,2,128,1]{0,2,3,1:T(8,128)(2,1)S(1)} %bitcast.63, f32[2,2,512,768]{2,3,1,0:T(8,128)} %get-tuple-element.57, f32[2,2,512]{2,1,0:T(2,128)S(1)} %get-tuple-element.56), kind=kOutput, calls=%fused_computation.17 | convolution fusion | flops 406061056 | bytes 7217152 | tf_op jit(solution)/shard_map/while/body/eval_jaxpr/gjrk,kgd->rgjd/dot_general | solution.py:82
  120.7 10.5 %all_to_all.24 = bf16[4,128,512]{1,2,0:T(8,128)(2,1)S(1)} all-to-all(bf16[4,128,512]{1,2,0:T(8,128)(2,1)S(1)} %copy.27), channel_id=1, replica_groups=mesh['seq'=64,'tp'=4] {'tp'}, dimensions={0} | all-to-all | bytes 1048576 | tf_op jit(solution)/shard_map/all_to_all | solution.py:144
  (56 shorter events, 7.9 us)
Async XLA Ops:
  0.6 64.9 %copy-start = (bf16[4096,256]{1,0:T(8,128)(2,1)S(1)}, bf16[4096,256]{1,0:T(8,128)(2,1)}, u32[]{:S(2)}) copy-start(bf16[4096,256]{1,0:T(8,128)(2,1)} %param.11) | copy-start | bytes 6291460
  4.5 5.0 %copy-start.5 = (s32[16]{0:T(128)S(1)}, s32[16]{0:T(128)}, u32[]{:S(2)}) copy-start(s32[16]{0:T(128)} %param.13) | copy-start | bytes 196
  4.5 10.9 %copy-start.4 = (s32[512]{0:T(512)S(1)}, s32[512]{0:T(512)}, u32[]{:S(2)}) copy-start(s32[512]{0:T(512)} %param.12) | copy-start | bytes 6148
  4.5 54.1 %all-to-all-start = ((bf16[4,128,4096]{2,1,0:T(8,128)(2,1)}), bf16[4,128,4096]{2,1,0:T(8,128)(2,1)}, u32[]{:S(2)}, u32[]{:S(2)}) async-start(bf16[4,128,4096]{2,1,0:T(8,128)(2,1)} %stack.2), calls=%async_computation | async-start | bytes 8388608 | tf_op jit(solution)/shard_map/all_to_all | solution.py:95
  9.7 19.0 %collective-permute-start.4 = (s32[128]{0:T(128)S(1)}, s32[128]{0:T(128)S(1)}, u32[]{:S(2)}, u32[]{:S(2)}) collective-permute-start(s32[128]{0:T(128)S(1)} %slice.56), channel_id=1, source_target_pairs={{4,0},{8,4},{12,8},{16,12},{20,16},{24,20},{28,24},{32,28},{36,32}... | collective-permute-start | bytes 1544 | tf_op jit(solution)/shard_map/ppermute | solution.py:16
  13.5 15.2 %collective-permute-start.3 = (s32[128]{0:T(128)S(1)}, s32[128]{0:T(128)S(1)}, u32[]{:S(2)}, u32[]{:S(2)}) collective-permute-start(s32[128]{0:T(128)S(1)} %slice.54), channel_id=1, source_target_pairs={{0,4},{4,8},{8,12},{12,16},{16,20},{20,24},{24,28},{28,32},{32,36}... | collective-permute-start | bytes 1544 | tf_op jit(solution)/shard_map/ppermute | solution.py:16
  15.5 13.3 %collective-permute-start.1 = (s32[512]{0:T(512)S(1)}, s32[512]{0:T(512)S(1)}, u32[]{:S(2)}, u32[]{:S(2)}) collective-permute-start(s32[512]{0:T(512)S(1)} %copy-done.4), channel_id=1, source_target_pairs={{0,4},{4,8},{8,12},{12,16},{16,20},{20,24},{24,28},{28,32},{32,36}... | collective-permute-start | bytes 6152 | tf_op jit(solution)/shard_map/ppermute | solution.py:16
  28.7 33.0 %copy-start.3 = (f32[4096]{0:T(1024)S(1)}, f32[4096]{0:T(1024)}, u32[]{:S(2)}) copy-start(f32[4096]{0:T(1024)} %param.8) | copy-start | bytes 49156
  67.5 41.1 %collective-permute-start = (bf16[512,256]{1,0:T(8,128)(2,1)S(1)}, bf16[512,256]{1,0:T(8,128)(2,1)}, u32[]{:S(2)}, u32[]{:S(2)}) collective-permute-start(bf16[512,256]{1,0:T(8,128)(2,1)S(1)} %convolution_convert_fusion), channel_id=1, source_target_pairs={{0,4},{4,8},{8,12},{12,16},{16,20},{20,24},{24,28},{28,32},{32,36}... | collective-permute-start | bytes 786440 | tf_op jit(solution)/shard_map/ppermute | solution.py:16
  69.4 4.0 %copy-start.2 = (bf16[256,4096]{1,0:T(8,128)(2,1)S(1)}, bf16[256,4096]{1,0:T(8,128)(2,1)}, u32[]{:S(2)}) copy-start(bf16[256,4096]{1,0:T(8,128)(2,1)} %copy.36) | copy-start | bytes 6291460
  73.4 2.0 %copy-start.1 = (bf16[4,128,4096]{2,1,0:T(8,128)(2,1)}, bf16[4,128,4096]{2,1,0:T(8,128)(2,1)S(1)}, u32[]{:S(2)}) copy-start(bf16[4,128,4096]{2,1,0:T(8,128)(2,1)S(1)} %multiply_convert_fusion) | copy-start | bytes 12582916
  75.4 24.2 %collective-permute-start.8 = (bf16[128,256]{1,0:T(8,128)(2,1)}, bf16[128,256]{1,0:T(8,128)(2,1)}, u32[]{:S(2)}, u32[]{:S(2)}) collective-permute-start(bf16[128,256]{1,0:T(8,128)(2,1)} %get-tuple-element.43), channel_id=1, source_target_pairs={{4,0},{8,4},{12,8},{16,12},{20,16},{24,20},{28,24},{32,28},{36,32}... | collective-permute-start | bytes 196616 | tf_op jit(solution)/shard_map/ppermute | solution.py:16
  82.4 20.2 %collective-permute-start.7 = (bf16[128,256]{1,0:T(8,128)(2,1)}, bf16[128,256]{1,0:T(8,128)(2,1)}, u32[]{:S(2)}, u32[]{:S(2)}) collective-permute-start(bf16[128,256]{1,0:T(8,128)(2,1)} %get-tuple-element.42), channel_id=1, source_target_pairs={{0,4},{4,8},{8,12},{12,16},{16,20},{20,24},{24,28},{28,32},{32,36}... | collective-permute-start | bytes 196616 | tf_op jit(solution)/shard_map/ppermute | solution.py:16
  84.5 24.1 %collective-permute-start.2 = (bf16[512,256]{1,0:T(8,128)(2,1)S(1)}, bf16[512,256]{1,0:T(8,128)(2,1)}, u32[]{:S(2)}, u32[]{:S(2)}) collective-permute-start(bf16[512,256]{1,0:T(8,128)(2,1)S(1)} %copy.37), channel_id=1, source_target_pairs={{0,4},{4,8},{8,12},{12,16},{16,20},{20,24},{24,28},{28,32},{32,36}... | collective-permute-start | bytes 786440 | tf_op jit(solution)/shard_map/ppermute | solution.py:16
  86.5 16.1 %collective-permute-start.6 = (bf16[128,256]{1,0:T(8,128)(2,1)S(1)}, bf16[128,256]{1,0:T(8,128)(2,1)}, u32[]{:S(2)}, u32[]{:S(2)}) collective-permute-start(bf16[128,256]{1,0:T(8,128)(2,1)S(1)} %copy.42), channel_id=1, source_target_pairs={{4,0},{8,4},{12,8},{16,12},{20,16},{24,20},{28,24},{32,28},{36,32}... | collective-permute-start | bytes 196616 | tf_op jit(solution)/shard_map/ppermute | solution.py:16
  99.6 8.9 %collective-permute-start.5 = (bf16[128,256]{1,0:T(8,128)(2,1)S(1)}, bf16[128,256]{1,0:T(8,128)(2,1)S(1)}, u32[]{:S(2)}, u32[]{:S(2)}) collective-permute-start(bf16[128,256]{1,0:T(8,128)(2,1)S(1)} %copy.41), channel_id=1, source_target_pairs={{0,4},{4,8},{8,12},{12,16},{16,20},{20,24},{24,28},{28,32},{32,36}... | collective-permute-start | bytes 196616 | tf_op jit(solution)/shard_map/ppermute | solution.py:16
